TPU v7x, 128 devices: a whole 4x4x4 slice. The times are simulated.
128 devices in a mesh: dp: 16 (over z, x), tensor: 8 (over y, core).
Axes of the slice: x: 4, y: 4, z: 4, core: 2. Of those that a mesh axis runs over, the one named last changes fastest.
Arguments:
- tokens: bfloat16 [128, 128, 8192], P('dp', None, 'tensor'), may hold values from -6 to 6
- shared_prefix_tokens: bfloat16 [16, 256, 8192], P('dp', None, 'tensor'), may hold values from -6 to 6
- input_norm_gain: bfloat16 [8192], replicated, may hold values from 0.5 to 8
- query_weight: bfloat16 [8192, 8192], P(None, 'tensor'), may hold values from -0.0625 to 0.0625
- key_weight: bfloat16 [8192, 1024], P(None, 'tensor'), may hold values from -0.0625 to 0.0625
- value_weight: bfloat16 [8192, 1024], P(None, 'tensor'), may hold values from -0.0625 to 0.0625
- adapter_down_weight: bfloat16 [64, 8192, 16], P('dp', 'tensor'), may hold values from -0.0625 to 0.0625
- adapter_up_weight: bfloat16 [64, 16, 8192], P('dp', None, 'tensor'), may hold values from -0.75 to 0.75
- adapter_position: int32 [64], replicated, may hold values from 0 to 63, as said below
- request_adapter: int32 [128], P('dp'), may hold values from 0 to 63, as said below
- request_group: int32 [128], P('dp'), may hold values from 0 to 15
- lengths: int32 [128], P('dp'), may hold values from 1 to 128
- request_page_table: int32 [128, 1], P('dp'), may hold values from 0 to 127, as said below
Outputs:
- context: bfloat16 [128, 128, 8192], P('dp', None, 'tensor')
- paged_key_values: bfloat16 [128, 2, 128, 1024], P('dp', None, None, 'tensor')
Inputs may be any that keep to these rules, and one draw needn't show every extreme that they name: A permutation: adapter a is held at slot adapter_position[a], on index adapter_position[a] // 4 of dp. `request_adapter`: the 8 requests of one index of dp use adapters held by 8 different indices of dp. `request_page_table`: the requests of index i of dp use the pages i * 8 to (i + 1) * 8 - 1, each page once.
All inputs are finite; a program needn't handle non-finite values.
Results may differ from a plain program's by a relative error of at most 0.011.
The roundings to bfloat16 on the way count: a program that leaves them out, or rounds other values in their place, can miss the bound.
Values may be sent and summed in bfloat16 or wider, within the bound.
No kernel may reach another device: no remote copies, remote signals or barrier semaphores. Data moves between devices by JAX's collectives and lax.ppermute only.
A program may use at most 128 MiB of HBM per device.

v0:
```python
import jax
import jax.numpy as jnp
from jax import lax
from jax.sharding import PartitionSpec as P

HEAD_WIDTH = 128
ADAPTER_RANK = 16
PAGE_TOKENS = 128
EPS = 1e-05
THETA = 500000.0
ADAPTER_SCALE = 2.0


def rope_tables(positions, width):
    half = width // 2
    freq = THETA ** (-(jnp.arange(half, dtype=jnp.float32) * 2.0 / width))
    angle = positions.astype(jnp.float32)[:, None] * freq[None, :]
    return (jnp.cos(angle), jnp.sin(angle))


def apply_rope(values, cosine, sine):
    half = values.shape[-1] // 2
    first = values[..., :half]
    second = values[..., half:]
    cos_b = cosine[:, None, :]
    sin_b = sine[:, None, :]
    return jnp.concatenate(
        [first * cos_b - second * sin_b, second * cos_b + first * sin_b], axis=-1
    )


def normalize(rows, gain):
    values = rows.astype(jnp.float32)
    scale = lax.rsqrt(jnp.mean(values * values, axis=-1, keepdims=True) + EPS)
    return (values * scale * gain.astype(jnp.float32)).astype(jnp.bfloat16)


def on_device(
    tokens,
    shared_prefix_tokens,
    input_norm_gain,
    query_weight,
    key_weight,
    value_weight,
    adapter_down_weight,
    adapter_up_weight,
    adapter_position,
    request_adapter,
    request_group,
    lengths,
    request_page_table,
):
    req_dev, seq_len, d_part = tokens.shape
    grp_dev, pre_len, _ = shared_prefix_tokens.shape
    q_width = query_weight.shape[1]
    kv_width = key_weight.shape[1]
    q_heads = q_width // HEAD_WIDTH
    kv_local = kv_width // HEAD_WIDTH
    group_members = q_heads // kv_local
    token_rows = req_dev * seq_len
    column = lax.axis_index("tensor")
    place = lax.axis_index("dp")
    full_tokens, full_prefix = (
        lax.all_gather(tokens.reshape(token_rows, d_part), "tensor", axis=1, tiled=True),
        lax.all_gather(
            shared_prefix_tokens.reshape(grp_dev * pre_len, d_part), "tensor", axis=1, tiled=True
        ),
    )
    normed_input = normalize(full_tokens, input_norm_gain)
    prefix_normed = normalize(full_prefix, input_norm_gain)
    pre_cos, pre_sin = rope_tables(jnp.arange(pre_len), HEAD_WIDTH)
    pre_keys = jnp.dot(prefix_normed, key_weight, preferred_element_type=jnp.float32).reshape(
        grp_dev, pre_len, kv_local, HEAD_WIDTH
    )
    pre_keys = (
        apply_rope(pre_keys, pre_cos, pre_sin)
        .astype(jnp.bfloat16)
        .reshape(grp_dev, pre_len, kv_width)
    )
    pre_vals = (
        jnp.dot(prefix_normed, value_weight, preferred_element_type=jnp.float32)
        .astype(jnp.bfloat16)
        .reshape(grp_dev, pre_len, kv_width)
    )
    all_pairs = lax.all_gather(jnp.stack([pre_keys, pre_vals], 1), "dp", axis=0, tiled=True)
    table_ids = jnp.arange(adapter_position.shape[0])
    slots = jnp.sum(
        jnp.where(request_adapter[:, None] == table_ids[None, :], adapter_position[None, :], 0),
        axis=1,
    )
    local_rows = lax.dynamic_slice_in_dim(normed_input, column * d_part, d_part, 1)
    row_slot = jnp.repeat(slots, seq_len)
    page_piece = lax.all_gather(adapter_down_weight, "dp", axis=0, tiled=True)
    count = page_piece.shape[0]
    part = jnp.einsum("td,ndr->tnr", local_rows, page_piece, preferred_element_type=jnp.float32)
    pick = row_slot[:, None] == jnp.arange(count)[None, :]
    partial_low = jnp.sum(jnp.where(pick[:, :, None], part, 0.0), axis=1)
    low_rank_rows = lax.psum(partial_low, "tensor").astype(jnp.bfloat16)
    page_piece = lax.all_gather(adapter_up_weight, "dp", axis=0, tiled=True)
    count = page_piece.shape[0]
    pick = (row_slot[:, None] == jnp.arange(count)[None, :]).astype(jnp.bfloat16)
    spread = (pick[:, :, None] * low_rank_rows[:, None, :]).reshape(
        token_rows, count * ADAPTER_RANK
    )
    summed_rows = jnp.dot(
        spread,
        page_piece.reshape(count * ADAPTER_RANK, q_width),
        preferred_element_type=jnp.float32,
    )
    adapter_term = (ADAPTER_SCALE * summed_rows).astype(jnp.bfloat16)
    own_cos, own_sin = rope_tables(pre_len + jnp.arange(seq_len), HEAD_WIDTH)
    query_rows = jnp.dot(
        normed_input, query_weight, preferred_element_type=jnp.float32
    ) + adapter_term.astype(jnp.float32)
    query_rows = apply_rope(
        query_rows.reshape(req_dev, seq_len, q_heads, HEAD_WIDTH), own_cos, own_sin
    ).astype(jnp.bfloat16)
    key_rows = jnp.dot(normed_input, key_weight, preferred_element_type=jnp.float32).reshape(
        req_dev, seq_len, kv_local, HEAD_WIDTH
    )
    key_rows = apply_rope(key_rows, own_cos, own_sin).astype(jnp.bfloat16)
    value_rows = (
        jnp.dot(normed_input, value_weight, preferred_element_type=jnp.float32)
        .astype(jnp.bfloat16)
        .reshape(req_dev, seq_len, kv_local, HEAD_WIDTH)
    )
    live = jnp.arange(seq_len)[None, :] < lengths[:, None]
    key_rows = jnp.where(live[:, :, None, None], key_rows, jnp.zeros_like(key_rows))
    value_rows = jnp.where(live[:, :, None, None], value_rows, jnp.zeros_like(value_rows))
    chosen = all_pairs[request_group]
    all_keys = jnp.concatenate(
        [chosen[:, 0].reshape(req_dev, pre_len, kv_local, HEAD_WIDTH), key_rows], 1
    )
    all_vals = jnp.concatenate(
        [chosen[:, 1].reshape(req_dev, pre_len, kv_local, HEAD_WIDTH), value_rows], 1
    )
    grouped_query = query_rows.reshape(req_dev, seq_len, kv_local, group_members, HEAD_WIDTH)
    scores = jnp.einsum(
        "btkgd,bskd->bkgts", grouped_query, all_keys, preferred_element_type=jnp.float32
    ) * HEAD_WIDTH ** (-0.5)
    seen = jnp.arange(pre_len + seq_len)[None, :]
    allowed = (seen < pre_len) | (seen - pre_len <= jnp.arange(seq_len)[:, None])
    scores = jnp.where(allowed[None, None, None], scores, -1e30)
    top = jnp.max(scores, axis=-1, keepdims=True)
    weights = jnp.exp(scores - top)
    probs = (weights / jnp.sum(weights, axis=-1, keepdims=True)).astype(jnp.bfloat16)
    attention_output = jnp.einsum(
        "bkgts,bskd->btkgd", probs, all_vals, preferred_element_type=jnp.float32
    )
    attention_output = jnp.where(live[:, :, None, None, None], attention_output, 0.0)
    context = attention_output.reshape(req_dev, seq_len, q_width).astype(jnp.bfloat16)
    pages_req = seq_len // PAGE_TOKENS
    page_blocks = jnp.stack(
        [
            key_rows.reshape(req_dev, pages_req, PAGE_TOKENS, kv_width),
            value_rows.reshape(req_dev, pages_req, PAGE_TOKENS, kv_width),
        ],
        2,
    )
    page_blocks = page_blocks.reshape(req_dev * pages_req, 2, PAGE_TOKENS, kv_width)
    local_page = request_page_table.reshape(-1) - place * (req_dev * pages_req)
    paged_key_values = jnp.zeros_like(page_blocks).at[local_page].set(page_blocks)
    return (context, paged_key_values)


def solution(mesh):
    in_specs = (
        P("dp", None, "tensor"),
        P("dp", None, "tensor"),
        P(),
        P(None, "tensor"),
        P(None, "tensor"),
        P(None, "tensor"),
        P("dp", "tensor", None),
        P("dp", None, "tensor"),
        P(),
        P("dp"),
        P("dp"),
        P("dp"),
        P("dp", None),
    )
    out_specs = (P("dp", None, "tensor"), P("dp", None, None, "tensor"))
    return jax.shard_map(
        on_device, mesh=mesh, in_specs=in_specs, out_specs=out_specs, check_vma=False
    )
```

profile of v0, /device:TPU:0, one launch (start us, length us, event | category | flops | bytes accessed | tf_op | source)
XLA Modules:
  0.0 344.5 jit_solution(120121396503228455)
XLA Ops:
  8.0 0.7 convert_element_type.114
  8.7 35.6 %all-gather.15.cloned.1.call-done = bf16[1,256,8192]{2,1,0:T(8,128)(2,1)} async-done(((bf16[1,256,1024]{2,1,0:T(8,128)(2,1)}), bf16[1,256,8192]{2,1,0:T(8,128)(2,1)}) %all-gather.15.cloned.1.call-update) | async-done | bytes 4194320 | tf_op jit(solution)/shard_map/all_gather | solution.py:65
  44.3 3.3 fusion.5
  47.8 3.3 fusion.33
  51.5 1.7 fusion.39
  53.3 0.8 copy.63
  58.6 40.8 %all-gather.7.cloned.1.call-done = bf16[16,2,256,128]{3,2,1,0:T(8,128)(2,1)} async-done(((bf16[1,2,256,128]{3,2,1,0:T(8,128)(2,1)}), bf16[16,2,256,128]{3,2,1,0:T(8,128)(2,1)}) %all-gather.7.cloned.1.call-update) | async-done | bytes 2097168 | tf_op jit(solution)/shard_map/all_gather | solution.py:85
  99.4 2.5 gather_fusion
  101.9 1.0 fusion.67
  102.9 2.0 copy.78
  105.0 80.4 %all-gather.9.cloned.1.call-done = bf16[1024,8192]{1,0:T(8,128)(2,1)} async-done(((bf16[1024,1024]{1,0:T(8,128)(2,1)}), bf16[1024,8192]{1,0:T(8,128)(2,1)}) %all-gather.9.cloned.1.call-update) | async-done | bytes 16777232 | tf_op jit(solution)/shard_map/all_gather | solution.py:64
  185.4 7.5 %fusion = f32[1024]{0:T(1024)S(1)} fusion(bf16[1024,8192]{1,0:T(8,128)(2,1)} %all-gather.9.cloned.1.call-done), kind=kLoop, calls=%fused_computation.4 | loop fusion | flops 25164800 | bytes 16781312 | tf_op jit(solution)/shard_map/reduce_sum | solution.py:34
  192.9 3.2 copy-done.2
  196.0 8.3 %fusion.2 = bf16[1024,8192]{1,0:T(8,128)(2,1)} fusion(bf16[1024,8192]{1,0:T(8,128)(2,1)S(1)} %copy-done.2, f32[8192]{0:T(1024)S(1)} %convert_element_type.114, f32[1024]{0:T(1024)S(1)} %add_rsqrt_fusion), kind=kLoop, calls=%fused_computation.6 | loop fusion | flops 33554432 | bytes 33591296 | tf_op jit(solution)/shard_map/convert_element_type | solution.py:35
  204.3 29.0 %all-gather.11.cloned.1.call-done = bf16[64,1024,16]{1,2,0:T(8,128)(2,1)} async-done(((bf16[4,1024,16]{1,2,0:T(8,128)(2,1)}), bf16[64,1024,16]{1,2,0:T(8,128)(2,1)}) %all-gather.11.cloned.1.call-update) | async-done | bytes 2097168 | tf_op jit(solution)/shard_map/all_gather | solution.py:93
  233.3 5.1 %select_reduce_fusion = f32[1024,16]{0,1:T(8,128)S(1)} fusion(pred[1024,64]{0,1:T(8,128)(4,1)S(1)} %get-tuple-element.23, bf16[64,1024,16]{1,2,0:T(8,128)(2,1)} %all-gather.11.cloned.1.call-done, bf16[1024,8192]{1,0:T(8,128)(2,1)} %fusion.2, s32[]{:T(128)S(6)} %select_n.72), kind=kOutput, calls=%fused_computation.27 | convolution fusion | flops 2149564416 | bytes 4325380 | tf_op jit(solution)/shard_map/td,ndr->tnr/dot_general | solution.py:95
  238.4 25.3 %psum.7 = bf16[1024,16]{0,1:T(8,128)(2,1)S(1)} all-reduce(f32[1024,16]{0,1:T(8,128)S(1)} %select_reduce_fusion), channel_id=1, replica_groups=mesh['dp'=16,'tensor'=8] {'tensor'}, use_global_device_ids=true, to_apply=%region_4.5 | all-reduce | flops 16384 | bytes 98304 | tf_op jit(solution)/shard_map/psum | solution.py:98
  263.7 8.5 %convolution_convert_fusion = bf16[1024,128]{1,0:T(8,128)(2,1)S(1)} fusion(bf16[1024,8192]{1,0:T(8,128)(2,1)} %fusion.2, bf16[8192,128]{1,0:T(8,128)(2,1)S(1)} %copy-done), kind=kOutput, calls=%fused_computation.38 | convolution fusion | flops 2147614720 | bytes 19136512 | tf_op jit(solution)/shard_map/dot_general | solution.py:123
  272.2 2.4 copy-done.3
  275.2 4.5 %fusion.68 = f32[1024,128]{1,0:T(8,128)S(1)} fusion(bf16[1024,8192]{1,0:T(8,128)(2,1)S(1)} %copy-done.3, bf16[8192,128]{1,0:T(8,128)(2,1)S(1)} %copy-done.11), kind=kOutput, calls=%fused_computation.101 | convolution fusion | flops 2147483648 | bytes 19398656 | tf_op jit(solution)/shard_map/dot_general | solution.py:118
  279.8 5.4 %fusion.12 = bf16[1024,1024]{1,0:T(8,128)(2,1)S(1)} fusion(bf16[64,16,1024]{2,1,0:T(8,128)(2,1)} %all-gather.13.cloned.1.call-done, bf16[1024,16]{0,1:T(8,128)(2,1)S(1)} %psum.7, bf16[1024,64]{0,1:T(8,128)(2,1)S(1)} %get-tuple-element.22), kind=kOutput, calls=%fused_computation.23 | convolution fusion | flops 2150629376 | bytes 4358144 | tf_op jit(solution)/shard_map/dot_general | solution.py:105
  285.3 22.6 %add_bitcast_fusion = f32[128,8,8,128]{3,1,2,0:T(8,128)S(1)} fusion(bf16[1024,1024]{1,0:T(8,128)(2,1)S(1)} %fusion.12, bf16[1024,8192]{1,0:T(8,128)(2,1)} %fusion.2, bf16[8192,1024]{1,0:T(8,128)(2,1)} %param.16), kind=kOutput, calls=%fused_computation.26 | convolution fusion | flops 17181966336 | bytes 39845888 | tf_op jit(solution)/shard_map/dot_general | solution.py:112
  307.9 1.0 copy.82
  308.9 4.6 %fusion.66 = (f32[8,128,8,64]{3,2,1,0:T(8,128)}, f32[8,128,8,64]{3,2,1,0:T(8,128)}) fusion(f32[8,128,8,128]{3,2,1,0:T(8,128)S(1)} %bitcast.99), kind=kLoop, calls=%fused_computation.99 | loop fusion | bytes 8388608 | tf_op jit(solution)/shard_map/slice | solution.py:23
  314.0 0.8 copy.65
  314.9 5.2 %subtract_convert_fusion = (bf16[8,128,8,64]{3,1,2,0:T(8,128)(2,1)S(1)}, bf16[8,128,8,64]{3,1,2,0:T(8,128)(2,1)S(1)}) fusion(f32[8,128,8,64]{3,2,1,0:T(8,128)} %get-tuple-element.15, f32[8,128,8,64]{3,2,1,0:T(8,128)} %get-tuple-element.14, f32[128,64]{1,0:T(8,128)S(1)} %get-tuple-element.29, f32[128,64]{1,0:T(8,128)S(1)} %get-tuple-element.28), kind=kLoop, calls=%fused_computation.25 | loop fusion | flops 4194304 | bytes 6356992 | tf_op jit(solution)/shard_map/convert.4
  320.1 3.1 fusion.4
  323.2 3.2 fusion.3
  326.5 5.3 %fusion.11 = bf16[8,1,128,8,128]{4,2,3,0,1:T(8,128)(2,1)} fusion(f32[8,8,128]{2,1,0:T(8,128)S(1)} %fusion.3, f32[8,8,128]{2,1,0:T(8,128)S(1)} %get-tuple-element.30, f32[8,384,128,8]{2,1,3,0:T(8,128)S(1)} %get-tuple-element.31, pred[128,384]{0,1:T(8,128)(4,1)S(1)} %fusion.48, pred[8,128]{1,0:T(8,128)(4,1)S(1)} %copy-done.9, ...), kind=kOutput, calls=%fused_computation.21 | convolution fusion | flops 824705024 | bytes 15582208 | tf_op jit(solution)/shard_map/bkgts,bskd->btkgd/dot_general | solution.py:147
  331.7 4.1 %copy.73 = bf16[8,128,1024]{2,1,0:T(8,128)(2,1)} copy(bf16[8,128,1024]{1,2,0:T(8,128)(2,1)} %bitcast.103) | data formatting | bytes 4194304
  336.3 0.9 scatter_fusion
  337.2 0.8 copy-done.6
  (66 shorter events, 7.6 us)
Async XLA Ops:
  7.2 44.3 %copy-start = (bf16[8192,128]{1,0:T(8,128)(2,1)S(1)}, bf16[8192,128]{1,0:T(8,128)(2,1)}, u32[]{:S(2)}) copy-start(bf16[8192,128]{1,0:T(8,128)(2,1)} %param.18) | copy-start | bytes 6291460
  7.2 37.2 %all-gather.15.cloned.1.call-start = ((), (), s32[]{:S(2)}) async-start(), calls=%async_computation.4 | async-start | bytes 4718592 | tf_op jit(solution)/shard_map/all_gather | solution.py:65
  7.9 91.5 %all-gather.7.cloned.1.call-start = ((), (), s32[]{:S(2)}) async-start(), calls=%async_computation | async-start | bytes 2228224 | tf_op jit(solution)/shard_map/all_gather | solution.py:85
  44.3 3.4 %copy-start.4 = (bf16[1,256,8192]{2,1,0:T(8,128)(2,1)S(1)}, bf16[1,256,8192]{2,1,0:T(8,128)(2,1)}, u32[]{:S(2)}) copy-start(bf16[1,256,8192]{2,1,0:T(8,128)(2,1)} %all-gather.15.cloned.1.call-done) | copy-start | bytes 12582916
  51.5 4.6 %copy-start.12 = (s32[64]{0:T(128)S(1)}, s32[64]{0:T(128)}, u32[]{:S(2)}) copy-start(s32[64]{0:T(128)} %param.21) | copy-start | bytes 772
  51.5 4.6 %copy-start.13 = (s32[8]{0:T(128)S(1)}, s32[8]{0:T(128)}, u32[]{:S(2)}) copy-start(s32[8]{0:T(128)} %param.22) | copy-start | bytes 100
  51.5 5.2 %copy-start.14 = (s32[8]{0:T(128)S(1)}, s32[8]{0:T(128)}, u32[]{:S(2)}) copy-start(s32[8]{0:T(128)} %param.24) | copy-start | bytes 100
  51.5 5.8 %copy-start.15 = (s32[8]{0:T(128)S(1)}, s32[8]{0:T(128)}, u32[]{:S(2)}) copy-start(s32[8]{0:T(128)} %param.23) | copy-start | bytes 100
  51.5 6.6 %copy-start.16 = (s32[8,1]{0,1:T(1,128)S(1)}, s32[8,1]{0,1:T(1,128)}, u32[]{:S(2)}) copy-start(s32[8,1]{0,1:T(1,128)} %param.25) | copy-start | bytes 100
  54.1 131.3 %all-gather.9.cloned.1.call-start = ((), (), s32[]{:S(2)}) async-start(), calls=%async_computation.1 | async-start | bytes 18874368 | tf_op jit(solution)/shard_map/all_gather | solution.py:64
  54.8 178.5 %all-gather.11.cloned.1.call-start = ((), (), s32[]{:S(2)}) async-start(), calls=%async_computation.2 | async-start | bytes 2228224 | tf_op jit(solution)/shard_map/all_gather | solution.py:93
  55.4 224.4 %all-gather.13.cloned.1.call-start = ((), (), s32[]{:S(2)}) async-start(), calls=%async_computation.3 | async-start | bytes 2228224 | tf_op jit(solution)/shard_map/all_gather | solution.py:99
  185.4 10.7 %copy-start.2 = (bf16[1024,8192]{1,0:T(8,128)(2,1)S(1)}, bf16[1024,8192]{1,0:T(8,128)(2,1)}, u32[]{:S(2)}) copy-start(bf16[1024,8192]{1,0:T(8,128)(2,1)} %all-gather.9.cloned.1.call-done) | copy-start | bytes 50331652
  263.7 10.9 %copy-start.3 = (bf16[1024,8192]{1,0:T(8,128)(2,1)S(1)}, bf16[1024,8192]{1,0:T(8,128)(2,1)}, u32[]{:S(2)}) copy-start(bf16[1024,8192]{1,0:T(8,128)(2,1)} %fusion.2) | copy-start | bytes 50331652
  263.7 11.5 %copy-start.11 = (bf16[8192,128]{1,0:T(8,128)(2,1)S(1)}, bf16[8192,128]{1,0:T(8,128)(2,1)}, u32[]{:S(2)}) copy-start(bf16[8192,128]{1,0:T(8,128)(2,1)} %param.17) | copy-start | bytes 6291460
  308.9 4.8 %copy-start.9 = (pred[8,128]{1,0:T(8,128)(4,1)S(1)}, pred[8,128]{1,0:T(8,128)(4,1)}, u32[]{:S(2)}) copy-start(pred[8,128]{1,0:T(8,128)(4,1)} %iota_compare_fusion.3) | copy-start | bytes 3076
  314.9 5.2 %copy-start.5 = (bf16[8,256,1,128]{3,1,0,2:T(8,128)(2,1)S(1)}, bf16[8,256,1,128]{3,1,0,2:T(8,128)(2,1)}, u32[]{:S(2)}) copy-start(bf16[8,256,1,128]{3,1,0,2:T(8,128)(2,1)} %get-tuple-element.17) | copy-start | bytes 1572868
  323.2 3.2 copy-start.7
  323.2 3.2 copy-start.8
  331.7 4.6 %copy-start.10 = (s32[8]{0:T(128)S(1)}, s32[8]{0:T(128)}, u32[]{:S(2)}) copy-start(s32[8]{0:T(128)} %fusion.59) | copy-start | bytes 100
  331.7 6.2 %copy-start.1 = (bf16[8192,128]{1,0:T(8,128)(2,1)S(1)}, bf16[8192,128]{1,0:T(8,128)(2,1)}, u32[]{:S(2)}) copy-start(bf16[8192,128]{1,0:T(8,128)(2,1)} %param.18) | copy-start | bytes 6291460
  337.2 0.8 copy-start.6
Sparse Core Ops, SparseCore 0:
  9.7 34.5 all-gather.14
  54.2 45.1 all-gather.6
  101.1 84.1 all-gather.8
  187.4 45.8 all-gather.10
  235.3 44.5 all-gather.12
where the time goes:
time: 345 us
  waiting for transfers between devices  188 us (54%)
  matrix products  59.5 us (17%)
  other arithmetic  31.9 us (9%)
  blocking collectives  25.3 us (7%)
  local copies, waits for them, and re-layouts  25.1 us (7%)
  between operations  14.2 us (4%)
    all_gather x1, waiting for transfers between devices, on_device(): lax.all_gather(tokens.reshape(token_rows, d_part), 'tensor', axis=1, tile...  80.4 us
    all_gather x1, waiting for transfers between devices, on_device(): lax.all_gather(jnp.stack([pre_keys, pre_vals], 1), 'dp', axis=0, tiled=True)  40.8 us
    all_gather x1, waiting for transfers between devices, on_device(): lax.all_gather(shared_prefix_tokens.reshape(grp_dev * pre_len, d_part), '...  35.6 us
    all_gather x1, waiting for transfers between devices, on_device(): page_piece = lax.all_gather(adapter_down_weight, 'dp', axis=0, tiled=True)  29 us
    psum x1, blocking collectives, on_device(): low_rank_rows = lax.psum(partial_low, 'tensor').astype(jnp.bfloat16)  25.3 us
    dot_general x1, matrix products, on_device(): jnp.dot(normed_input, query_weight, preferred_element_type=jnp.float32)  22.6 us
    unnamed x37, local copies, waits for them, and re-layouts  14.3 us
    reduce_sum x2, other arithmetic, normalize(): scale = lax.rsqrt(jnp.mean(values * values, axis=-1, keepdims=True) + EPS)  10.7 us
  transfers between devices with their start and end apart: 5, of which 5 were waited for; matrix products, arithmetic and copies ran while one was open for 12% of the time, Pallas kernels for 0%

commit v1 on v0

--- a/solution.py
+++ b/solution.py
@@ -95,7 +95,7 @@
     part = jnp.einsum("td,ndr->tnr", local_rows, page_piece, preferred_element_type=jnp.float32)
     pick = row_slot[:, None] == jnp.arange(count)[None, :]
     partial_low = jnp.sum(jnp.where(pick[:, :, None], part, 0.0), axis=1)
-    low_rank_rows = lax.psum(partial_low, "tensor").astype(jnp.bfloat16)
+    low_rank_rows = jnp.sum(lax.all_gather(partial_low, "tensor"), axis=0).astype(jnp.bfloat16)
     page_piece = lax.all_gather(adapter_up_weight, "dp", axis=0, tiled=True)
     count = page_piece.shape[0]
     pick = (row_slot[:, None] == jnp.arange(count)[None, :]).astype(jnp.bfloat16)

time: 345 us -> 361 us (1.046); the launches traced: 345 us -> 354 us
  waiting for transfers between devices: 188 us -> 206 us
  blocking collectives: 25.3 us -> 14 us
  matrix products: 59.5 us -> 65.4 us
    psum x1 -> x0, blocking collectives: 25.3 us -> none  [on_device(): low_rank_rows = lax.psum(partial_low, 'tensor').astype(jnp.bfloat16)]
    all_gather x1, waiting for transfers between devices: 0.15 us -> 17.9 us  [on_device(): page_piece = lax.all_gather(adapter_up_weight, 'dp', axis=0, tiled=True)]
    all_gather x0 -> x1, blocking collectives: none -> 14 us  [on_device(): lax.all_gather(partial_low, 'tensor')]
    dot_general x1, matrix products: 22.6 us -> 32.4 us  [on_device(): jnp.dot(normed_input, query_weight, preferred_element_type=jnp.float32)]
    dot_general x1, matrix products: 8.46 us -> 4.5 us  [on_device(): jnp.dot(normed_input, value_weight, preferred_element_type=jnp.float32)]
    unnamed x37 -> x38, local copies, waits for them, and re-layouts: 14.3 us -> 11.6 us
  transfers between devices with their start and end apart: 5 -> 5, of which waited for: 5 -> 5; matrix products, arithmetic and copies ran while one was open for 12% -> 11% of each run, Pallas kernels for 0% -> 0%
where the time goes in v1:
time: 361 us; the launch traced here: 354 us
  waiting for transfers between devices  206 us (57%)
  matrix products  65.4 us (18%)
  other arithmetic  32 us (9%)
  local copies, waits for them, and re-layouts  22.4 us (6%)
  between operations  14.4 us (4%)
  blocking collectives  14 us (4%)
    all_gather x1, waiting for transfers between devices, on_device(): lax.all_gather(tokens.reshape(token_rows, d_part), 'tensor', axis=1, tile...  80.4 us
    all_gather x1, waiting for transfers between devices, on_device(): lax.all_gather(jnp.stack([pre_keys, pre_vals], 1), 'dp', axis=0, tiled=True)  40.8 us
    all_gather x1, waiting for transfers between devices, on_device(): lax.all_gather(shared_prefix_tokens.reshape(grp_dev * pre_len, d_part), '...  35.6 us
    dot_general x1, matrix products, on_device(): jnp.dot(normed_input, query_weight, preferred_element_type=jnp.float32)  32.4 us
    all_gather x1, waiting for transfers between devices, on_device(): page_piece = lax.all_gather(adapter_down_weight, 'dp', axis=0, tiled=True)  29 us
    all_gather x1, waiting for transfers between devices, on_device(): page_piece = lax.all_gather(adapter_up_weight, 'dp', axis=0, tiled=True)  17.9 us
    all_gather x1, blocking collectives, on_device(): lax.all_gather(partial_low, 'tensor')  14 us
    unnamed x38, local copies, waits for them, and re-layouts  11.6 us
  transfers between devices with their start and end apart: 5, of which 5 were waited for; matrix products, arithmetic and copies ran while one was open for 11% of the time, Pallas kernels for 0%

profile of v1, /device:TPU:0, one launch (start us, length us, event | category | flops | bytes accessed | tf_op | source)
XLA Modules:
  0.0 354.4 jit_solution(11165510129076116435)
XLA Ops:
  8.0 0.7 convert_element_type.118
  8.7 35.6 %all-gather.16.cloned.1.call-done = bf16[1,256,8192]{2,1,0:T(8,128)(2,1)} async-done(((bf16[1,256,1024]{2,1,0:T(8,128)(2,1)}), bf16[1,256,8192]{2,1,0:T(8,128)(2,1)}) %all-gather.16.cloned.1.call-update) | async-done | bytes 4194320 | tf_op jit(solution)/shard_map/all_gather | solution.py:65
  44.3 3.3 fusion.5
  47.8 3.3 fusion.33
  51.5 1.7 fusion.39
  53.3 0.8 copy.63
  58.6 40.8 %all-gather.8.cloned.1.call-done = bf16[16,2,256,128]{3,2,1,0:T(8,128)(2,1)} async-done(((bf16[1,2,256,128]{3,2,1,0:T(8,128)(2,1)}), bf16[16,2,256,128]{3,2,1,0:T(8,128)(2,1)}) %all-gather.8.cloned.1.call-update) | async-done | bytes 2097168 | tf_op jit(solution)/shard_map/all_gather | solution.py:85
  99.4 2.5 gather_fusion
  101.9 1.0 fusion.67
  102.9 2.0 copy.78
  105.0 80.4 %all-gather.10.cloned.1.call-done = bf16[1024,8192]{1,0:T(8,128)(2,1)} async-done(((bf16[1024,1024]{1,0:T(8,128)(2,1)}), bf16[1024,8192]{1,0:T(8,128)(2,1)}) %all-gather.10.cloned.1.call-update) | async-done | bytes 16777232 | tf_op jit(solution)/shard_map/all_gather | solution.py:64
  185.4 7.5 %fusion = f32[1024]{0:T(1024)S(1)} fusion(bf16[1024,8192]{1,0:T(8,128)(2,1)} %all-gather.10.cloned.1.call-done), kind=kLoop, calls=%fused_computation.4 | loop fusion | flops 25164800 | bytes 16781312 | tf_op jit(solution)/shard_map/reduce_sum | solution.py:34
  192.9 3.2 copy-done.2
  196.0 8.3 %fusion.2 = bf16[1024,8192]{1,0:T(8,128)(2,1)} fusion(bf16[1024,8192]{1,0:T(8,128)(2,1)S(1)} %copy-done.2, f32[8192]{0:T(1024)S(1)} %convert_element_type.118, f32[1024]{0:T(1024)S(1)} %add_rsqrt_fusion), kind=kLoop, calls=%fused_computation.6 | loop fusion | flops 33554432 | bytes 33591296 | tf_op jit(solution)/shard_map/convert_element_type | solution.py:35
  204.3 29.0 %all-gather.12.cloned.1.call-done = bf16[64,1024,16]{1,2,0:T(8,128)(2,1)} async-done(((bf16[4,1024,16]{1,2,0:T(8,128)(2,1)}), bf16[64,1024,16]{1,2,0:T(8,128)(2,1)}) %all-gather.12.cloned.1.call-update) | async-done | bytes 2097168 | tf_op jit(solution)/shard_map/all_gather | solution.py:93
  233.3 5.2 %select_reduce_fusion = f32[1024,16]{0,1:T(8,128)S(1)} fusion(pred[1024,64]{0,1:T(8,128)(4,1)S(1)} %get-tuple-element.23, bf16[64,1024,16]{1,2,0:T(8,128)(2,1)} %all-gather.12.cloned.1.call-done, bf16[1024,8192]{1,0:T(8,128)(2,1)} %fusion.2, s32[]{:T(128)S(6)} %select_n.72), kind=kOutput, calls=%fused_computation.27 | convolution fusion | flops 2149564416 | bytes 4325380 | tf_op jit(solution)/shard_map/td,ndr->tnr/dot_general | solution.py:95
  238.5 14.0 %all-gather.1 = f32[8192,16]{0,1:T(8,128)S(1)} all-gather(f32[1024,16]{0,1:T(8,128)S(1)} %select_reduce_fusion), channel_id=3, replica_groups=mesh['dp'=16,'tensor'=8] {'tensor'}, dimensions={0}, use_global_device_ids=true | all-gather | bytes 589824 | tf_op jit(solution)/shard_map/all_gather | solution.py:98
  253.0 4.5 %convolution_convert_fusion = bf16[1024,128]{1,0:T(8,128)(2,1)S(1)} fusion(bf16[1024,8192]{1,0:T(8,128)(2,1)S(1)} %copy-done.3, bf16[8192,128]{1,0:T(8,128)(2,1)S(1)} %copy-done), kind=kOutput, calls=%fused_computation.38 | convolution fusion | flops 2147614720 | bytes 19136512 | tf_op jit(solution)/shard_map/dot_general | solution.py:123
  257.5 4.5 %fusion.68 = f32[1024,128]{1,0:T(8,128)S(1)} fusion(bf16[1024,8192]{1,0:T(8,128)(2,1)S(1)} %copy-done.3, bf16[8192,128]{1,0:T(8,128)(2,1)S(1)} %copy-done.11), kind=kOutput, calls=%fused_computation.102 | convolution fusion | flops 2147483648 | bytes 19398656 | tf_op jit(solution)/shard_map/dot_general | solution.py:118
  262.0 17.9 %all-gather.14.cloned.1.call-done = bf16[64,16,1024]{2,1,0:T(8,128)(2,1)} async-done(((bf16[4,16,1024]{2,1,0:T(8,128)(2,1)}), bf16[64,16,1024]{2,1,0:T(8,128)(2,1)}) %all-gather.14.cloned.1.call-update) | async-done | bytes 2097168 | tf_op jit(solution)/shard_map/all_gather | solution.py:99
  279.8 5.4 %fusion.12 = bf16[1024,1024]{1,0:T(8,128)(2,1)S(1)} fusion(bf16[64,16,1024]{2,1,0:T(8,128)(2,1)} %all-gather.14.cloned.1.call-done, bf16[1024,16]{0,1:T(8,128)(2,1)S(1)} %bitcast_reduce_fusion, bf16[1024,64]{0,1:T(8,128)(2,1)S(1)} %get-tuple-element.22), kind=kOutput, calls=%fused_computation.23 | convolution fusion | flops 2150629376 | bytes 4358144 | tf_op jit(solution)/shard_map/dot_general | solution.py:105
  285.3 32.4 %add_bitcast_fusion = f32[128,8,8,128]{3,1,2,0:T(8,128)S(1)} fusion(bf16[1024,1024]{1,0:T(8,128)(2,1)S(1)} %fusion.12, bf16[1024,8192]{1,0:T(8,128)(2,1)} %fusion.2, bf16[8192,1024]{1,0:T(8,128)(2,1)} %param.16), kind=kOutput, calls=%fused_computation.26 | convolution fusion | flops 17181966336 | bytes 39845888 | tf_op jit(solution)/shard_map/dot_general | solution.py:112
  317.7 1.0 copy.83
  318.7 4.6 %fusion.66 = (f32[8,128,8,64]{3,2,1,0:T(8,128)}, f32[8,128,8,64]{3,2,1,0:T(8,128)}) fusion(f32[8,128,8,128]{3,2,1,0:T(8,128)S(1)} %bitcast.104), kind=kLoop, calls=%fused_computation.100 | loop fusion | bytes 8388608 | tf_op jit(solution)/shard_map/slice | solution.py:23
  323.8 0.8 copy.65
  324.7 5.2 %subtract_convert_fusion = (bf16[8,128,8,64]{3,1,2,0:T(8,128)(2,1)S(1)}, bf16[8,128,8,64]{3,1,2,0:T(8,128)(2,1)S(1)}) fusion(f32[8,128,8,64]{3,2,1,0:T(8,128)} %get-tuple-element.15, f32[8,128,8,64]{3,2,1,0:T(8,128)} %get-tuple-element.14, f32[128,64]{1,0:T(8,128)S(1)} %get-tuple-element.29, f32[128,64]{1,0:T(8,128)S(1)} %get-tuple-element.28), kind=kLoop, calls=%fused_computation.25 | loop fusion | flops 4194304 | bytes 6356992 | tf_op jit(solution)/shard_map/convert.4
  329.9 3.1 fusion.4
  333.0 3.2 fusion.3
  336.2 5.2 %fusion.11 = bf16[8,1,128,8,128]{4,2,3,0,1:T(8,128)(2,1)} fusion(f32[8,8,128]{2,1,0:T(8,128)S(1)} %fusion.3, f32[8,8,128]{2,1,0:T(8,128)S(1)} %get-tuple-element.30, f32[8,384,128,8]{2,1,3,0:T(8,128)S(1)} %get-tuple-element.31, pred[128,384]{0,1:T(8,128)(4,1)S(1)} %fusion.48, pred[8,128]{1,0:T(8,128)(4,1)S(1)} %copy-done.9, ...), kind=kOutput, calls=%fused_computation.21 | convolution fusion | flops 824705024 | bytes 15582208 | tf_op jit(solution)/shard_map/bkgts,bskd->btkgd/dot_general | solution.py:147
  341.5 4.1 %copy.73 = bf16[8,128,1024]{2,1,0:T(8,128)(2,1)} copy(bf16[8,128,1024]{1,2,0:T(8,128)(2,1)} %bitcast.108) | data formatting | bytes 4194304
  346.0 0.9 scatter_fusion
  346.9 0.8 copy-done.6
  (68 shorter events, 7.3 us)
Async XLA Ops:
  7.2 44.3 %copy-start = (bf16[8192,128]{1,0:T(8,128)(2,1)S(1)}, bf16[8192,128]{1,0:T(8,128)(2,1)}, u32[]{:S(2)}) copy-start(bf16[8192,128]{1,0:T(8,128)(2,1)} %param.18) | copy-start | bytes 6291460
  7.2 37.2 %all-gather.16.cloned.1.call-start = ((), (), s32[]{:S(2)}) async-start(), calls=%async_computation.4 | async-start | bytes 4718592 | tf_op jit(solution)/shard_map/all_gather | solution.py:65
  7.9 91.5 %all-gather.8.cloned.1.call-start = ((), (), s32[]{:S(2)}) async-start(), calls=%async_computation | async-start | bytes 2228224 | tf_op jit(solution)/shard_map/all_gather | solution.py:85
  44.3 3.4 copy-start.4
  51.5 4.6 %copy-start.12 = (s32[64]{0:T(128)S(1)}, s32[64]{0:T(128)}, u32[]{:S(2)}) copy-start(s32[64]{0:T(128)} %param.21) | copy-start | bytes 772
  51.5 4.6 %copy-start.13 = (s32[8]{0:T(128)S(1)}, s32[8]{0:T(128)}, u32[]{:S(2)}) copy-start(s32[8]{0:T(128)} %param.22) | copy-start | bytes 100
  51.5 5.2 %copy-start.14 = (s32[8]{0:T(128)S(1)}, s32[8]{0:T(128)}, u32[]{:S(2)}) copy-start(s32[8]{0:T(128)} %param.24) | copy-start | bytes 100
  51.5 5.8 %copy-start.15 = (s32[8]{0:T(128)S(1)}, s32[8]{0:T(128)}, u32[]{:S(2)}) copy-start(s32[8]{0:T(128)} %param.23) | copy-start | bytes 100
  51.5 6.6 %copy-start.16 = (s32[8,1]{0,1:T(1,128)S(1)}, s32[8,1]{0,1:T(1,128)}, u32[]{:S(2)}) copy-start(s32[8,1]{0,1:T(1,128)} %param.25) | copy-start | bytes 100
  54.1 131.3 %all-gather.10.cloned.1.call-start = ((), (), s32[]{:S(2)}) async-start(), calls=%async_computation.1 | async-start | bytes 18874368 | tf_op jit(solution)/shard_map/all_gather | solution.py:64
  54.8 178.5 %all-gather.12.cloned.1.call-start = ((), (), s32[]{:S(2)}) async-start(), calls=%async_computation.2 | async-start | bytes 2228224 | tf_op jit(solution)/shard_map/all_gather | solution.py:93
  55.4 224.4 %all-gather.14.cloned.1.call-start = ((), (), s32[]{:S(2)}) async-start(), calls=%async_computation.3 | async-start | bytes 2228224 | tf_op jit(solution)/shard_map/all_gather | solution.py:99
  185.4 10.7 %copy-start.2 = (bf16[1024,8192]{1,0:T(8,128)(2,1)S(1)}, bf16[1024,8192]{1,0:T(8,128)(2,1)}, u32[]{:S(2)}) copy-start(bf16[1024,8192]{1,0:T(8,128)(2,1)} %all-gather.10.cloned.1.call-done) | copy-start | bytes 50331652
  233.3 19.7 %copy-start.3 = (bf16[1024,8192]{1,0:T(8,128)(2,1)S(1)}, bf16[1024,8192]{1,0:T(8,128)(2,1)}, u32[]{:S(2)}) copy-start(bf16[1024,8192]{1,0:T(8,128)(2,1)} %fusion.2) | copy-start | bytes 50331652
  253.0 4.5 %copy-start.11 = (bf16[8192,128]{1,0:T(8,128)(2,1)S(1)}, bf16[8192,128]{1,0:T(8,128)(2,1)}, u32[]{:S(2)}) copy-start(bf16[8192,128]{1,0:T(8,128)(2,1)} %param.17) | copy-start | bytes 6291460
  318.7 4.8 %copy-start.9 = (pred[8,128]{1,0:T(8,128)(4,1)S(1)}, pred[8,128]{1,0:T(8,128)(4,1)}, u32[]{:S(2)}) copy-start(pred[8,128]{1,0:T(8,128)(4,1)} %iota_compare_fusion.3) | copy-start | bytes 3076
  324.7 5.2 %copy-start.5 = (bf16[8,256,1,128]{3,1,0,2:T(8,128)(2,1)S(1)}, bf16[8,256,1,128]{3,1,0,2:T(8,128)(2,1)}, u32[]{:S(2)}) copy-start(bf16[8,256,1,128]{3,1,0,2:T(8,128)(2,1)} %get-tuple-element.17) | copy-start | bytes 1572868
  333.0 3.2 copy-start.7
  333.0 3.2 copy-start.8
  341.5 4.6 %copy-start.10 = (s32[8]{0:T(128)S(1)}, s32[8]{0:T(128)}, u32[]{:S(2)}) copy-start(s32[8]{0:T(128)} %fusion.59) | copy-start | bytes 100
  341.5 6.2 %copy-start.1 = (bf16[8192,128]{1,0:T(8,128)(2,1)S(1)}, bf16[8192,128]{1,0:T(8,128)(2,1)}, u32[]{:S(2)}) copy-start(bf16[8192,128]{1,0:T(8,128)(2,1)} %param.18) | copy-start | bytes 6291460
  346.9 0.8 copy-start.6
Sparse Core Ops, SparseCore 0:
  9.7 34.5 all-gather.15
  54.2 45.1 all-gather.7
  101.1 84.1 all-gather.9
  187.4 45.8 all-gather.11
  235.3 44.5 all-gather.13
